TPU v7x, 32 devices: a whole 2x2x4 slice. The times are simulated.
32 devices in a mesh: layer: 4 (over y, x), lat: 8 (over z, core).
Axes of the slice: x: 2, y: 2, z: 4, core: 2. Of those that a mesh axis runs over, the one named last changes fastest.
Arguments:
- inputs: bfloat16 [4, 1, 5120, 128], P(None, None, 'lat'), may hold values from -6 to 6
- encoder: bfloat16 [4, 8192, 5120], P('layer', 'lat'), may hold values from -0.125 to 0.125
- decoder: bfloat16 [4, 4, 8192, 5120], P('layer', None, 'lat'), may hold values from -0.09375 to 0.09375
- encoder_bias: float32 [4, 8192], P(None, 'lat'), may hold values from -3 to 3
- tile_mask: int32 [4, 64, 128], P(None, 'lat'), may hold values 0 or 1
- targets: bfloat16 [1, 5120, 4, 128], P(None, 'lat'), may hold values from -6 to 6
- decoder_bias: float32 [1, 5120, 4], P(None, 'lat'), may hold values from -3 to 3
Outputs:
- errors: bfloat16 [1, 5120, 4, 128], P(None, 'lat')
- input_grads: bfloat16 [4, 5120, 128], P('layer', 'lat')
All inputs are finite; a program needn't handle non-finite values. No bound on the sum of `tile_mask` on one device may be relied on, other than what follows from the above.
Results may differ from a plain program's by a relative error of at most 0.0065.
Values may be sent and summed in bfloat16 or wider, within the bound.
A program may use at most 192 MiB of HBM per device.

v0:
```python
import jax
import jax.numpy as jnp
from jax import lax
from jax.sharding import PartitionSpec as P

TILE = 128


def over_sources(values):
    return lax.psum(values, "layer")


def run_blocks(totals, source_row, blocks, base_target, low_target, high_target, update):

    def advance(target, current):
        weights = lax.dynamic_index_in_dim(blocks, target - base_target, 0, keepdims=False)
        return update(current, target, source_row, weights)

    return lax.fori_loop(low_target, high_target, advance, totals)


def per_device(inputs, encoder, decoder, encoder_bias, tile_mask, targets, decoder_bias):
    layer_count = lax.axis_size("layer")
    lat_count = lax.axis_size("lat")
    layers = decoder.shape[1]
    quarters = layer_count // layers
    position = lax.axis_index("layer")
    source = position // quarters
    quarter = position % quarters
    encoder_rows = encoder[0]
    own_blocks = decoder[0]
    local_latents = encoder_rows.shape[0]
    quarter_width = encoder_rows.shape[1]
    kept_width = quarter_width // lat_count
    row_count = inputs.shape[3]
    block_jobs = [(source, own_blocks, 0, source, layers)]

    def run_all(totals, update):
        block_job = block_jobs[0]
        totals = run_blocks(
            totals, block_job[0], block_job[1], block_job[2], block_job[3], block_job[4], update
        )
        return totals

    own_input = lax.dynamic_index_in_dim(
        inputs.reshape((layers * quarters,) + inputs.shape[2:]), position, 0, keepdims=False
    )
    full_input = lax.all_gather(own_input, "lat", axis=0, tiled=True)
    own_preacts = jnp.dot(encoder_rows, full_input, preferred_element_type=jnp.float32)
    tile_count = tile_mask.shape[1]
    support = jnp.broadcast_to(
        tile_mask[:, :, None, :].astype(jnp.float32), (layers, tile_count, TILE, row_count)
    ).reshape(layers, local_latents, row_count)
    own_support = lax.dynamic_index_in_dim(support, source, 0, keepdims=False)
    source_slots = lax.dynamic_update_index_in_dim(
        jnp.zeros((layers, local_latents, row_count), jnp.float32), own_preacts, source, 0
    )
    preacts = over_sources(source_slots) + encoder_bias[:, :, None]
    activity = (jnp.maximum(preacts, 0.0) * support).astype(jnp.bfloat16)

    def forward_term():

        def update(current, target, source_row, weights):
            latent = lax.dynamic_index_in_dim(activity, source_row, 0, keepdims=False)
            contrib = lax.dot_general(
                weights, latent, (((0,), (0,)), ((), ())), preferred_element_type=jnp.float32
            )
            before = lax.dynamic_index_in_dim(current, target, 1, keepdims=False)
            return lax.dynamic_update_index_in_dim(current, before + contrib, target, 1)

        return run_all(
            jnp.zeros((kept_width * lax.axis_size("lat"), layers, row_count), jnp.float32), update
        )

    partial_value = lax.psum_scatter(forward_term(), "lat", scatter_dimension=0, tiled=True)
    placed = lax.dynamic_update_index_in_dim(
        jnp.zeros((quarters,) + partial_value.shape, jnp.float32), partial_value, quarter, 0
    )
    summed = over_sources(placed)
    errors = (summed + decoder_bias[:, :, :, None] - targets.astype(jnp.float32)).astype(
        jnp.bfloat16
    )
    own_errors = lax.dynamic_index_in_dim(errors, quarter, 0, keepdims=False)

    def fold_errors(totals, portion):

        def update(current, target, source_row, weights):
            error_rows = lax.dynamic_index_in_dim(portion, target, 1, keepdims=False)
            contrib = jnp.dot(weights, error_rows, preferred_element_type=jnp.float32)
            before = lax.dynamic_index_in_dim(current, source_row, 0, keepdims=False)
            return lax.dynamic_update_index_in_dim(current, before + contrib, source_row, 0)

        return run_all(totals, update)

    latent_sums = fold_errors(
        jnp.zeros((layers, local_latents, row_count), jnp.float32),
        lax.all_gather(own_errors, "lat", axis=0, tiled=True),
    )
    latent_grad = over_sources(latent_sums)
    own_latent = lax.dynamic_index_in_dim(latent_grad, source, 0, keepdims=False)
    own_grad = (own_latent * own_support).astype(jnp.bfloat16)
    gradients = lax.psum_scatter(
        lax.dot_general(
            encoder_rows, own_grad, (((0,), (0,)), ((), ())), preferred_element_type=jnp.float32
        ),
        "lat",
        scatter_dimension=0,
        tiled=True,
    )
    return (errors, gradients.astype(jnp.bfloat16)[None])


def solution(mesh):
    in_specs = (
        P(None, None, "lat", None),
        P("layer", "lat", None),
        P("layer", None, "lat", None),
        P(None, "lat"),
        P(None, "lat", None),
        P(None, "lat", None, None),
        P(None, "lat", None),
    )
    out_specs = (P(None, "lat", None, None), P("layer", "lat", None))
    return jax.shard_map(
        per_device, mesh=mesh, in_specs=in_specs, out_specs=out_specs, check_vma=False
    )
```

profile of v0, /device:TPU:0, one launch (start us, length us, event | category | flops | bytes accessed | tf_op | source)
XLA Modules:
  0.0 923.1 jit_solution(17247908552409753957)
XLA Ops:
  7.2 1.0 copy-done
  8.3 0.7 constant_dynamic-slice_fusion.3
  9.0 27.4 %all-gather.5.cloned.1.call-done = bf16[1,1,5120,128]{3,2,1,0:T(8,128)(2,1)} async-done(((bf16[1,1,640,128]{3,2,1,0:T(8,128)(2,1)}), bf16[1,1,5120,128]{3,2,1,0:T(8,128)(2,1)}) %all-gather.5.cloned.1.call-update) | async-done | bytes 1310736 | tf_op jit(solution)/shard_map/all_gather | solution.py:48
  36.4 8.0 fusion.37
  44.4 0.2 copy.18
  44.6 0.1 broadcast.8.clone
  44.8 1.3 copy-done.3
  46.2 0.7 constant_dynamic-slice_fusion.2
  46.9 68.4 %all-reduce.6.cloned.1.call-done = f32[4,1024,128]{2,1,0:T(8,128)} async-done(((f32[4,1024,128]{2,1,0:T(8,128)}), f32[4,1024,128]{2,1,0:T(8,128)}) %all-reduce.6.cloned.1.call-update) | async-done | bytes 2097168 | tf_op jit(solution)/shard_map/psum | solution.py:10
  115.3 0.1 broadcast_in_dim.37
  115.4 1.3 copy-done.4
  116.8 1.2 fusion.44
  118.0 4.8 broadcast_in_dim.35.clone
  122.8 315.8 %while.24 = (s32[]{:T(128)}, f32[5120,4,128]{2,1,0:T(4,128)}, bf16[4,1024,5120]{2,1,0:T(8,128)(2,1)}, bf16[1,1024,128]{2,1,0:T(8,128)(2,1)S(1)}, s32[]{:T(128)}, /*index=5*/s32[]{:T(128)}, s32[]{:T(128)}) while((s32[]{:T(128)}, f32[5120,4,128]{2,1,0:T(4,128)}, bf16[4,1024,5120]{2,1,0:T(8,128)(2,1)}, bf16[1,1024,128]{2,1,0:T(8,128)(2,1)S(1)}, ...), condition=%wide.region_2.3_spmd, body=%wide.region_1.2_spmd.sunk | while | flops 1342832640 | bytes 26476668 | solution.py:19
  122.8 6.3 constant_dynamic-slice_fusion.6
  129.1 5.8 fusion.56
  134.8 66.9 %dynamic_update_slice.23 = f32[5120,4,128]{2,1,0:T(4,128)} dynamic-update-slice(f32[5120,4,128]{2,1,0:T(4,128)} %get-tuple-element.226, f32[5120,1,128]{2,1,0:T(1,128)S(1)} %bitcast.87, s32[]{:T(128)} %constant.114.clone.1..sunk, s32[]{:T(128)S(6)} %select_n.50, s32[]{:T(128)} %constant.114.clone.1..sunk) | dynamic-update-slice | bytes 5242884 | tf_op jit(solution)/shard_map/while/body/jit(dynamic_update_index_in_dim)/dynamic_update_slice | solution.py:69
  201.7 6.3 constant_dynamic-slice_fusion.6
  208.0 5.8 fusion.56
  213.8 66.9 %dynamic_update_slice.23 = f32[5120,4,128]{2,1,0:T(4,128)} dynamic-update-slice(f32[5120,4,128]{2,1,0:T(4,128)} %get-tuple-element.226, f32[5120,1,128]{2,1,0:T(1,128)S(1)} %bitcast.87, s32[]{:T(128)} %constant.114.clone.1..sunk, s32[]{:T(128)S(6)} %select_n.50, s32[]{:T(128)} %constant.114.clone.1..sunk) | dynamic-update-slice | bytes 5242884 | tf_op jit(solution)/shard_map/while/body/jit(dynamic_update_index_in_dim)/dynamic_update_slice | solution.py:69
  280.7 6.3 constant_dynamic-slice_fusion.6
  287.0 5.8 fusion.56
  292.7 66.9 %dynamic_update_slice.23 = f32[5120,4,128]{2,1,0:T(4,128)} dynamic-update-slice(f32[5120,4,128]{2,1,0:T(4,128)} %get-tuple-element.226, f32[5120,1,128]{2,1,0:T(1,128)S(1)} %bitcast.87, s32[]{:T(128)} %constant.114.clone.1..sunk, s32[]{:T(128)S(6)} %select_n.50, s32[]{:T(128)} %constant.114.clone.1..sunk) | dynamic-update-slice | bytes 5242884 | tf_op jit(solution)/shard_map/while/body/jit(dynamic_update_index_in_dim)/dynamic_update_slice | solution.py:69
  359.6 6.3 constant_dynamic-slice_fusion.6
  365.9 5.8 fusion.56
  371.7 66.9 %dynamic_update_slice.23 = f32[5120,4,128]{2,1,0:T(4,128)} dynamic-update-slice(f32[5120,4,128]{2,1,0:T(4,128)} %get-tuple-element.226, f32[5120,1,128]{2,1,0:T(1,128)S(1)} %bitcast.87, s32[]{:T(128)} %constant.114.clone.1..sunk, s32[]{:T(128)S(6)} %select_n.50, s32[]{:T(128)} %constant.114.clone.1..sunk) | dynamic-update-slice | bytes 5242884 | tf_op jit(solution)/shard_map/while/body/jit(dynamic_update_index_in_dim)/dynamic_update_slice | solution.py:69
  438.6 0.0 all-reduce.8.cloned.1.call-start
  438.7 0.6 copy-done.8
  439.2 0.6 dynamic-slice.1
  440.5 212.4 %all-reduce.12.cloned.1.call-done = f32[5120,4,128]{2,1,0:T(4,128)} async-done(((f32[5120,4,128]{2,1,0:T(4,128)}), f32[5120,4,128]{2,1,0:T(4,128)}) %all-reduce.12.cloned.1.call-update) | async-done | bytes 10485776
  652.9 2.5 dynamic-slice_bitcast_fusion
  655.4 0.2 copy.20
  655.6 56.7 %all-reduce.8.cloned.1.call-done = f32[1,640,4,128]{3,2,1,0:T(4,128)} async-done(((f32[1,640,4,128]{3,2,1,0:T(4,128)}), f32[1,640,4,128]{3,2,1,0:T(4,128)}) %all-reduce.8.cloned.1.call-update) | async-done | bytes 1310736 | tf_op jit(solution)/shard_map/psum | solution.py:10
  712.3 2.6 subtract_convert_fusion
  715.1 56.1 %all-gather.7.cloned.1.call-done = bf16[1,5120,4,128]{3,2,0,1:T(4,128)(2,1)} async-done(((bf16[1,640,4,128]{3,2,0,1:T(4,128)(2,1)}), bf16[1,5120,4,128]{3,2,0,1:T(4,128)(2,1)}) %all-gather.7.cloned.1.call-update) | async-done | bytes 5242896 | tf_op jit(solution)/shard_map/all_gather | solution.py:97
  771.1 5.5 copy.22
  776.6 0.1 broadcast.8
  776.7 24.3 %while.25 = (s32[]{:T(128)}, f32[4,1024,128]{2,1,0:T(8,128)S(1)}, s32[]{:T(128)}, bf16[4,1024,5120]{2,1,0:T(8,128)(2,1)}, bf16[5120,4,128]{2,0,1:T(8,128)(2,1)}, /*index=5*/s32[]{:T(128)}, s32[]{:T(128)}, s32[]{:T(128)}) while((s32[]{:T(128)}, f32[4,1024,128]{2,1,0:T(8,128)S(1)}, s32[]{:T(128)}, bf16[4,1024,5120]{2,1,0:T(8,128)(2,1)}, ...), condition=%wide.region_6.7_spmd, body=%wide.region_5.6_spmd.sunk | while | flops 1342308352 | bytes 13895291 | solution.py:19
  776.8 6.0 fusion.59
  782.9 6.0 fusion.59
  789.0 6.0 fusion.59
  795.1 6.0 fusion.59
  801.1 1.3 copy-done.2
  802.5 66.5 %all-reduce.10.cloned.1.call-done = f32[4,1024,128]{2,1,0:T(8,128)} async-done(((f32[4,1024,128]{2,1,0:T(8,128)}), f32[4,1024,128]{2,1,0:T(8,128)}) %all-reduce.10.cloned.1.call-update) | async-done | bytes 2097168 | tf_op jit(solution)/shard_map/psum | solution.py:10
  869.0 7.4 fusion.33
  876.5 38.0 %reduce-scatter.2.cloned.1.call-done = f32[640,128]{0,1:T(8,128)} async-done(((f32[5120,128]{0,1:T(8,128)}), f32[640,128]{0,1:T(8,128)}) %reduce-scatter.2.cloned.1.call-update) | async-done | bytes 327696 | tf_op jit(solution)/shard_map/reduce_scatter | solution.py:102
  914.5 1.0 convert_bitcast_fusion
  915.5 0.8 copy.23
  (32 shorter events, 0.6 us)
Async XLA Ops:
  7.2 1.1 copy-start
  7.2 29.2 %all-gather.5.cloned.1.call-start = ((), (), s32[]{:S(2)}) async-start(), calls=%async_computation.5 | async-start | bytes 1474560 | tf_op jit(solution)/shard_map/all_gather | solution.py:48
  9.0 106.3 %all-reduce.6.cloned.1.call-start = ((), (), s32[]{:S(2)}) async-start(), calls=%async_computation.1 | async-start | bytes 4194304 | tf_op jit(solution)/shard_map/psum | solution.py:10
  44.6 1.6 copy-start.6
  44.8 1.3 copy-start.3
  46.1 606.8 %all-reduce.12.cloned.1.call-start = ((), (), s32[]{:S(2)}) async-start(), calls=%async_computation.7 | async-start | bytes 20971520
  115.4 1.4 copy-start.4
  438.6 0.7 copy-start.8
  438.6 216.8 %copy-start.7 = (f32[1,640,4]{1,2,0:T(4,128)S(1)}, f32[1,640,4]{1,2,0:T(4,128)}, u32[]{:S(2)}) copy-start(f32[1,640,4]{1,2,0:T(4,128)} %param.17) | copy-start | bytes 30724
  438.6 273.7 %copy-start.5 = (bf16[1,640,4,128]{3,2,1,0:T(4,128)(2,1)S(1)}, bf16[1,640,4,128]{3,2,1,0:T(4,128)(2,1)}, u32[]{:S(2)}) copy-start(bf16[1,640,4,128]{3,2,1,0:T(4,128)(2,1)} %param.16) | copy-start | bytes 1966084
  438.6 273.7 %all-reduce.8.cloned.1.call-start = ((), (), s32[]{:S(2)}) async-start(), calls=%async_computation.2 | async-start | bytes 2621440 | tf_op jit(solution)/shard_map/psum | solution.py:10
  655.4 115.8 %all-gather.7.cloned.1.call-start = ((), (), s32[]{:S(2)}) async-start(), calls=%async_computation.6 | async-start | bytes 5898240 | tf_op jit(solution)/shard_map/all_gather | solution.py:97
  715.0 154.0 %all-reduce.10.cloned.1.call-start = ((), (), s32[]{:S(2)}) async-start(), calls=%async_computation.3 | async-start | bytes 4194304 | tf_op jit(solution)/shard_map/psum | solution.py:10
  801.1 1.3 copy-start.2
  802.5 112.0 %reduce-scatter.2.cloned.1.call-start = ((), (), s32[]{:S(2)}) async-start(), calls=%async_computation.4 | async-start | bytes 2949120 | tf_op jit(solution)/shard_map/reduce_scatter | solution.py:102
  869.0 47.3 %copy-start.1 = (bf16[4,1,640,128]{3,2,1,0:T(8,128)(2,1)S(1)}, bf16[4,1,640,128]{3,2,1,0:T(8,128)(2,1)}, u32[]{:S(2)}) copy-start(bf16[4,1,640,128]{3,2,1,0:T(8,128)(2,1)} %param.11) | copy-start | bytes 1966084
Sparse Core Ops, SparseCore 0:
  10.2 26.1 all-gather.4
  46.2 68.9 all-reduce.5
  438.7 214.1 all-reduce.11
  655.8 56.4 all-reduce.7
  715.1 55.9 all-gather.6
  802.6 66.3 all-reduce.9
  876.6 37.8 reduce-scatter.1
where the time goes:
time: 930 us; the launch traced here: 923 us
  waiting for transfers between devices  526 us (57%)
  local copies, waits for them, and re-layouts  315 us (34%)
  matrix products  62.5 us (7%)
  between operations  14.9 us (2%)
    dynamic_update_slice x4, local copies, waits for them, and re-layouts, update(): return lax.dynamic_update_index_in_dim(current, before + contrib, target, 1)  268 us
    unnamed x8, waiting for transfers between devices  213 us
    psum x3, waiting for transfers between devices, over_sources(): return lax.psum(values, 'layer')  192 us
    all_gather x1, waiting for transfers between devices, per_device(): lax.all_gather(own_errors, 'lat', axis=0, tiled=True)  56.1 us
    reduce_scatter x1, waiting for transfers between devices, per_device(): lax.psum_scatter(lax.dot_general(encoder_rows, own_grad, (((0,), (0,)), (...  38 us
    all_gather x1, waiting for transfers between devices, per_device(): full_input = lax.all_gather(own_input, 'lat', axis=0, tiled=True)  27.4 us
    dynamic_slice x4, local copies, waits for them, and re-layouts, update(): before = lax.dynamic_index_in_dim(current, target, 1, keepdims=False)  25 us
    dot_general x4, matrix products, update(): contrib = jnp.dot(weights, error_rows, preferred_element_type=jnp.float32)  24 us
  transfers between devices with their start and end apart: 7, of which 7 were waited for; matrix products, arithmetic and copies ran while one was open for 0% of the time, Pallas kernels for 0%

commit v1 on v0

--- a/solution.py
+++ b/solution.py
@@ -1,6 +1,8 @@
 import jax
 import jax.numpy as jnp
 from jax import lax
+from jax.experimental import pallas as pl
+from jax.experimental.pallas import tpu as pltpu
 from jax.sharding import PartitionSpec as P
 
 TILE = 128
@@ -110,7 +112,164 @@
     return (errors, gradients.astype(jnp.bfloat16)[None])
 
 
+def width_tile(width):
+    tile = width
+    while tile > 1280 and tile % 256 == 0:
+        tile //= 2
+    return tile
+
+
+def forward_kernel(first_ref, latent_ref, weights_ref, out_ref):
+    active = pl.program_id(0) >= first_ref[0]
+
+    @pl.when(active)
+    def _():
+        term = jnp.dot(latent_ref[...], weights_ref[0], preferred_element_type=jnp.float32)
+        out_ref[...] = term.T.astype(out_ref.dtype)
+
+    @pl.when(jnp.logical_not(active))
+    def _():
+        out_ref[...] = jnp.zeros_like(out_ref)
+
+
+def spread(first, latent_t, weights, dtype):
+    blocks, latents, width = weights.shape
+    rows = latent_t.shape[0]
+    tile = width_tile(width)
+    return pl.pallas_call(
+        forward_kernel,
+        out_shape=jax.ShapeDtypeStruct((width, blocks * rows), dtype),
+        grid_spec=pltpu.PrefetchScalarGridSpec(
+            num_scalar_prefetch=1,
+            grid=(blocks, width // tile),
+            in_specs=[
+                pl.BlockSpec((rows, latents), lambda t, d, first: (0, 0)),
+                pl.BlockSpec(
+                    (1, latents, tile),
+                    lambda t, d, first: (
+                        jnp.maximum(t, first[0]), 0, jnp.where(t < first[0], 0, d)
+                    ),
+                ),
+            ],
+            out_specs=pl.BlockSpec((tile, rows), lambda t, d, first: (d, t)),
+        ),
+        cost_estimate=pl.CostEstimate(
+            flops=2 * blocks * latents * width * rows,
+            bytes_accessed=2 * blocks * latents * width,
+            transcendentals=0,
+        ),
+    )(first, latent_t, weights)
+
+
+def backward_kernel(first_ref, weights_ref, errors_ref, support_ref, out_ref, total):
+    target, part = pl.program_id(0), pl.program_id(1)
+
+    @pl.when((target == 0) & (part == 0))
+    def _():
+        total[...] = jnp.zeros_like(total)
+
+    @pl.when(target >= first_ref[0])
+    def _():
+        total[...] += jnp.dot(
+            weights_ref[0], errors_ref[...], preferred_element_type=jnp.float32
+        )
+
+    @pl.when((target == pl.num_programs(0) - 1) & (part == pl.num_programs(1) - 1))
+    def _():
+        out_ref[...] = (total[...] * support_ref[...]).T.astype(out_ref.dtype)
+
+
+def gather_back(first, weights, errors, support):
+    blocks, latents, width = weights.shape
+    rows = support.shape[1]
+    tile = width_tile(width)
+
+    def block_of(t, first):
+        return jnp.maximum(t, first[0])
+
+    def part_of(t, d, first):
+        return jnp.where(t < first[0], 0, d)
+
+    return pl.pallas_call(
+        backward_kernel,
+        out_shape=jax.ShapeDtypeStruct((rows, latents), jnp.bfloat16),
+        grid_spec=pltpu.PrefetchScalarGridSpec(
+            num_scalar_prefetch=1,
+            grid=(blocks, width // tile),
+            in_specs=[
+                pl.BlockSpec(
+                    (1, latents, tile),
+                    lambda t, d, first: (block_of(t, first), 0, part_of(t, d, first)),
+                ),
+                pl.BlockSpec(
+                    (tile, rows),
+                    lambda t, d, first: (part_of(t, d, first), block_of(t, first)),
+                ),
+                pl.BlockSpec((latents, rows), lambda t, d, first: (0, 0)),
+            ],
+            out_specs=pl.BlockSpec((rows, latents), lambda t, d, first: (0, 0)),
+            scratch_shapes=[pltpu.VMEM((latents, rows), jnp.float32)],
+        ),
+        cost_estimate=pl.CostEstimate(
+            flops=2 * blocks * latents * width * rows,
+            bytes_accessed=2 * blocks * latents * width,
+            transcendentals=0,
+        ),
+    )(first, weights, errors, support)
+
+
+def per_device_whole_width(
+    inputs, encoder, decoder, encoder_bias, tile_mask, targets, decoder_bias
+):
+    layers = decoder.shape[1]
+    position = lax.axis_index("layer")
+    lat = lax.axis_index("lat")
+    encoder_rows = encoder[0]
+    latents = encoder_rows.shape[0]
+    rows = inputs.shape[3]
+    kept = targets.shape[1]
+    piece = kept // layers
+    first = position.astype(jnp.int32)[None]
+
+    def own(values):
+        return lax.dynamic_index_in_dim(values, position, 0, keepdims=False)
+
+    full_input = lax.all_gather(own(inputs)[0], "lat", axis=0, tiled=True)
+    support = jnp.broadcast_to(
+        own(tile_mask)[:, None, :].astype(jnp.float32), (latents // TILE, TILE, rows)
+    ).reshape(latents, rows)
+    preacts = jnp.dot(encoder_rows, full_input, preferred_element_type=jnp.float32)
+    preacts = preacts + own(encoder_bias)[:, None]
+    activity_t = (jnp.maximum(preacts, 0.0) * support).astype(jnp.bfloat16).T
+    partial_value = spread(first, activity_t, decoder[0], jnp.bfloat16)
+    lat_sum = lax.psum_scatter(partial_value, "lat", scatter_dimension=0, tiled=True)
+    summed = lax.psum_scatter(
+        lat_sum.astype(jnp.float32), "layer", scatter_dimension=0, tiled=True
+    ).reshape(piece, layers, rows)
+    start = position * piece
+    own_targets = lax.dynamic_slice_in_dim(targets[0], start, piece, 0)
+    own_bias = lax.dynamic_slice_in_dim(decoder_bias[0], start, piece, 0)
+    own_errors = (
+        summed + own_bias[:, :, None] - own_targets.astype(jnp.float32)
+    ).astype(jnp.bfloat16).reshape(piece, layers * rows)
+    full_errors = lax.all_gather(own_errors, ("lat", "layer"), axis=0, tiled=True)
+    errors = lax.dynamic_slice_in_dim(full_errors, lat * kept, kept, 0)
+    own_grad_t = gather_back(first, decoder[0], full_errors, support)
+    gradients = lax.psum_scatter(
+        spread(jnp.zeros((1,), jnp.int32), own_grad_t, encoder, jnp.float32),
+        "lat",
+        scatter_dimension=0,
+        tiled=True,
+    )
+    return (errors.reshape(1, kept, layers, rows), gradients.astype(jnp.bfloat16)[None])
+
+
 def solution(mesh):
+    def run(*arrays):
+        if lax.axis_size("layer") == arrays[2].shape[1]:
+            return per_device_whole_width(*arrays)
+        return per_device(*arrays)
+
     in_specs = (
         P(None, None, "lat", None),
         P("layer", "lat", None),
@@ -122,5 +281,5 @@
     )
     out_specs = (P(None, "lat", None, None), P("layer", "lat", None))
     return jax.shard_map(
-        per_device, mesh=mesh, in_specs=in_specs, out_specs=out_specs, check_vma=False
-    )
+        run, mesh=mesh, in_specs=in_specs, out_specs=out_specs, check_vma=False
+    )

time: 930 us -> 300 us (0.32)
  waiting for transfers between devices: 526 us -> 210 us
  local copies, waits for them, and re-layouts: 315 us -> 6.58 us
  matrix products: 62.5 us -> 7.39 us
  Pallas kernels: 0 us -> 53.8 us
    dynamic_update_slice x5 -> x0, local copies, waits for them, and re-layouts: 268 us -> none  [the longest x4 268 us: update(): return lax.dynamic_update_index_in_dim(current, before + contrib, target, 1)]
    unnamed x8 -> x5, waiting for transfers between devices: 213 us -> 0.08 us
    psum x3 -> x0, waiting for transfers between devices: 192 us -> none  [over_sources(): return lax.psum(values, 'layer')]
    reduce_scatter x1 -> x3, waiting for transfers between devices: 38 us -> 118 us  [the longest x1 57.7 us: per_device_whole_width(): lax.psum_scatter(partial_value, 'lat', scatter_dimension=0, tiled=True)]
    dot_general x10 -> x1, matrix products: 62.5 us -> 7.39 us  [per_device_whole_width(): jnp.dot(encoder_rows, full_input, preferred_element_type=jnp.float32)]
    pallas_call x0 -> x3, Pallas kernels: none -> 53.8 us  [the longest x2 29.6 us: spread(): pl.pallas_call(forward_kernel, out_shape=jax.ShapeDtypeStruct((width, blo...]
    dynamic_slice x10 -> x3, local copies, waits for them, and re-layouts: 26.6 us -> 2.53 us  [the longest x2 1.4 us: own(): return lax.dynamic_index_in_dim(values, position, 0, keepdims=False)]
  transfers between devices with their start and end apart: 7 -> 5, of which waited for: 7 -> 5; matrix products, arithmetic and copies ran while one was open for 0% -> 2% of each run, Pallas kernels for 0% -> 0%
where the time goes in v1:
time: 300 us; the launch traced here: 299 us
  waiting for transfers between devices  210 us (70%)
  Pallas kernels  53.8 us (18%)
  between operations  13.8 us (5%)
  matrix products  7.39 us (2%)
  other arithmetic  7.36 us (2%)
  local copies, waits for them, and re-layouts  6.58 us (2%)
    all_gather x1, waiting for transfers between devices, per_device_whole_width(): lax.all_gather(own_errors, ('lat', 'layer'), axis=0, tiled=True)  66.6 us
    reduce_scatter x1, waiting for transfers between devices, per_device_whole_width(): lax.psum_scatter(partial_value, 'lat', scatter_dimension=0, tiled=True)  57.7 us
    reduce_scatter x1, waiting for transfers between devices, per_device_whole_width(): lax.psum_scatter(spread(jnp.zeros((1,), jnp.int32), own_grad_t, encoder,...  33.4 us
    pallas_call x2, Pallas kernels, spread(): pl.pallas_call(forward_kernel, out_shape=jax.ShapeDtypeStruct((width, blo...  29.6 us
    reduce_scatter x1, waiting for transfers between devices, per_device_whole_width(): lax.psum_scatter(lat_sum.astype(jnp.float32), 'layer', scatter_dimension=...  26.6 us
    all_gather x1, waiting for transfers between devices, per_device_whole_width(): full_input = lax.all_gather(own(inputs)[0], 'lat', axis=0, tiled=True)  25.9 us
    pallas_call x1, Pallas kernels, gather_back(): pl.pallas_call(backward_kernel, out_shape=jax.ShapeDtypeStruct((rows, lat...  24.2 us
    dot_general x1, matrix products, per_device_whole_width(): jnp.dot(encoder_rows, full_input, preferred_element_type=jnp.float32)  7.39 us
  transfers between devices with their start and end apart: 5, of which 5 were waited for; matrix products, arithmetic and copies ran while one was open for 2% of the time, Pallas kernels for 0%

profile of v1, /device:TPU:0, one launch (start us, length us, event | category | flops | bytes accessed | tf_op | source)
XLA Modules:
  0.0 299.4 jit_solution(5936803147330510368)
XLA Ops:
  7.2 0.0 copy-start
  7.2 0.0 all-gather.6.cloned.1.call-start
  7.2 1.0 copy-done
  8.3 0.7 constant_dynamic-slice_fusion.2
  8.9 0.0 all-gather.6.cloned.1.call-update
  9.0 0.0 reduce-scatter.4.cloned.1.call-start
  9.0 0.7 convert_bitcast_fusion.1
  9.7 0.7 constant_dynamic-slice_fusion.1
  10.4 25.9 %all-gather.6.cloned.1.call-done = bf16[1,1,5120,128]{3,2,1,0:T(8,128)(2,1)} async-done(((bf16[1,1,640,128]{3,2,1,0:T(8,128)(2,1)}), bf16[1,1,5120,128]{3,2,1,0:T(8,128)(2,1)}) %all-gather.6.cloned.1.call-update) | async-done | bytes 1310736 | tf_op jit(solution)/shard_map/all_gather | solution.py:237
  36.4 0.0 copy-start.2
  36.4 7.4 %fusion.28 = bf16[128,1024]{0,1:T(8,128)(2,1)S(1)} fusion(f32[1024,128]{1,0:T(8,128)S(1)} %bitcast.63, bf16[1,1,5120,128]{3,2,1,0:T(8,128)(2,1)} %all-gather.6.cloned.1.call-done, bf16[1,1024,5120]{2,1,0:T(8,128)(2,1)} %weights_ref.1, f32[1024]{0:T(1024)S(1)} %bitcast.67), kind=kOutput, calls=%fused_computation.8 | convolution fusion | flops 1342701568 | bytes 12587008 | tf_op jit(solution)/shard_map/dot_general | solution.py:241
  43.8 0.0 copy-done.2
  43.8 0.9 copy.12.latent_ref
  44.7 22.6 %shard_map.86 = bf16[5120,512]{1,0:T(8,128)(2,1)} custom-call(s32[1]{0:T(128)} %bitcast.first_ref, bf16[128,1024]{1,0:T(8,128)(2,1)} %copy.12.latent_ref, bf16[4,1024,5120]{2,1,0:T(8,128)(2,1)} %bitcast.61), custom_call_target="tpu_custom_call" | custom-call | flops 5368709120 | bytes 41943040 | tf_op jit(solution)/shard_map/pallas_call | solution.py:139
  67.3 0.0 reduce-scatter.4.cloned.1.call-update
  67.3 0.0 reduce-scatter.6.cloned.1.call-start
  67.3 57.7 %reduce-scatter.4.cloned.1.call-done = bf16[640,512]{1,0:T(8,128)(2,1)} async-done(((bf16[5120,512]{1,0:T(8,128)(2,1)}), bf16[640,512]{1,0:T(8,128)(2,1)}) %reduce-scatter.4.cloned.1.call-update) | async-done | bytes 655376 | tf_op jit(solution)/shard_map/reduce_scatter | solution.py:245
  125.0 2.3 convert_element_type.34
  127.3 0.0 reduce-scatter.6.cloned.1.call-update
  127.4 0.0 all-gather.4.cloned.1.call-start
  127.4 0.8 dynamic-slice_bitcast_fusion
  128.2 0.1 copy.13
  128.3 1.0 dynamic-slice_convert_fusion
  129.3 26.6 %reduce-scatter.6.cloned.1.call-done = f32[160,512]{1,0:T(8,128)} async-done(((f32[640,512]{1,0:T(8,128)}), f32[160,512]{1,0:T(8,128)}) %reduce-scatter.6.cloned.1.call-update) | async-done | bytes 327696 | tf_op jit(solution)/shard_map/reduce_scatter | solution.py:246
  155.9 0.2 add.51
  156.1 1.7 fusion.33
  157.8 0.0 all-gather.4.cloned.1.call-update
  157.9 0.0 reduce-scatter.8.cloned.1.call-start
  157.9 66.6 %all-gather.4.cloned.1.call-done.errors_ref = bf16[5120,512]{1,0:T(8,128)(2,1)} async-done(((bf16[160,512]{1,0:T(8,128)(2,1)}), bf16[5120,512]{1,0:T(8,128)(2,1)}) %all-gather.4.cloned.1.call-update) | async-done | bytes 5242896 | tf_op jit(solution)/shard_map/all_gather | solution.py:255
  224.5 24.2 %shard_map.87.latent_ref = bf16[128,1024]{1,0:T(8,128)(2,1)} custom-call(s32[1]{0:T(128)} %bitcast.first_ref, bf16[4,1024,5120]{2,1,0:T(8,128)(2,1)} %bitcast.62, bf16[5120,512]{1,0:T(8,128)(2,1)} %all-gather.4.cloned.1.call-done.errors_ref, f32[1024,128]{1,0:T(8,128)} %bitcast.64), custom_call_target="tpu_custom_call" | custom-call | flops 5368709120 | bytes 41943040 | tf_op jit(solution)/shard_map/pallas_call | solution.py:193
  248.7 0.0 copy-start.1
  248.7 7.0 %shard_map.88 = f32[5120,128]{1,0:T(8,128)} custom-call(s32[1]{0:T(128)} %constant.34.clone.1.first_ref, bf16[128,1024]{1,0:T(8,128)(2,1)} %shard_map.87.latent_ref, bf16[1,1024,5120]{2,1,0:T(8,128)(2,1)} %weights_ref.1), custom_call_target="tpu_custom_call" | custom-call | flops 1342177280 | bytes 10485760 | tf_op jit(solution)/shard_map/pallas_call | solution.py:139
  255.7 0.0 reduce-scatter.8.cloned.1.call-update
  255.7 1.1 constant_dynamic-slice_fusion
  256.8 1.0 reshape.33
  257.8 33.4 %reduce-scatter.8.cloned.1.call-done = f32[640,128]{1,0:T(8,128)} async-done(((f32[5120,128]{1,0:T(8,128)}), f32[640,128]{1,0:T(8,128)}) %reduce-scatter.8.cloned.1.call-update) | async-done | bytes 327696 | tf_op jit(solution)/shard_map/reduce_scatter | solution.py:258
  291.3 1.7 convert_bitcast_fusion
  292.9 0.0 copy-done.1
  (1 shorter events, 0.0 us)
Async XLA Ops:
  7.2 1.1 copy-start
  7.2 29.2 %all-gather.6.cloned.1.call-start = ((), (), s32[]{:S(2)}) async-start(), calls=%async_computation.7 | async-start | bytes 1474560 | tf_op jit(solution)/shard_map/all_gather | solution.py:237
  9.0 116.0 %reduce-scatter.4.cloned.1.call-start = ((), (), s32[]{:S(2)}) async-start(), calls=%async_computation.3 | async-start | bytes 5898240 | tf_op jit(solution)/shard_map/reduce_scatter | solution.py:245
  36.4 7.4 %copy-start.2 = (f32[8,128,128]{2,1,0:T(8,128)}, f32[8,128,128]{2,1,0:T(8,128)S(1)}, u32[]{:S(2)}) copy-start(f32[8,128,128]{2,1,0:T(8,128)S(1)} %broadcast_in_dim.7) | copy-start | bytes 1572868
  67.3 88.6 %reduce-scatter.6.cloned.1.call-start = ((), (), s32[]{:S(2)}) async-start(), calls=%async_computation.4 | async-start | bytes 1638400 | tf_op jit(solution)/shard_map/reduce_scatter | solution.py:246
  127.4 97.1 %all-gather.4.cloned.1.call-start = ((), (), s32[]{:S(2)}) async-start(), calls=%async_computation.5 | async-start | bytes 5406720 | tf_op jit(solution)/shard_map/all_gather | solution.py:255
  157.9 133.4 %reduce-scatter.8.cloned.1.call-start = ((), (), s32[]{:S(2)}) async-start(), calls=%async_computation.6 | async-start | bytes 2949120 | tf_op jit(solution)/shard_map/reduce_scatter | solution.py:258
  248.7 44.2 %copy-start.1 = (bf16[4,1,640,128]{3,2,1,0:T(8,128)(2,1)S(1)}, bf16[4,1,640,128]{3,2,1,0:T(8,128)(2,1)}, u32[]{:S(2)}) copy-start(bf16[4,1,640,128]{3,2,1,0:T(8,128)(2,1)} %param.7) | copy-start | bytes 1966084
Sparse Core Ops, SparseCore 0:
  10.2 26.1 all-gather.5
  67.4 57.5 reduce-scatter.3
  127.9 27.9 reduce-scatter.5
  159.2 65.2 all-gather.3
  255.8 35.3 reduce-scatter.7
